TPU v7x, 768 devices: a whole 4x8x12 slice. The times are simulated.
768 devices in a mesh: axial: 48 (over z_lo, y, core), radial: 16 (over z_hi, x).
Axes of the slice: x: 4, y: 8, z: 12 (z_hi: 4, z_lo: 3; z = z_hi * 3 + z_lo), core: 2. Of those that a mesh axis runs over, the one named last changes fastest.
Arguments:
- species: float32 [5, 384, 128, 128], P(None, 'axial', 'radial')
- velocity: float32 [3, 384, 128, 128], P(None, 'axial', 'radial'), may hold values from -4 to 4
- diffusivity: float32 [384, 128, 128], P('axial', 'radial'), may hold values from 0.3 to 1
- parcels: float32 [48, 16, 16, 2048], P('axial', 'radial')
- counts: int32 [48, 16], P('axial', 'radial'), may hold values from 256 to 2048, as said below
- cells: int32 [48, 16, 2048], P('axial', 'radial'), may hold values from 0 to 8191, as said below
- leave_slots: int32 [48, 16, 4, 64], P('axial', 'radial'), may hold values from 0 to 2047, as said below
- leave_counts: int32 [48, 16, 4], P('axial', 'radial'), may hold values from 16 to 64, as said below
Outputs:
- species_out: float32 [5, 384, 128, 128], P(None, 'axial', 'radial')
- velocity_out: float32 [3, 384, 128, 128], P(None, 'axial', 'radial')
- staying: float32 [48, 16, 16, 2048], P('axial', 'radial')
- arrivals: float32 [48, 16, 4, 16, 64], P('axial', 'radial')
Inputs may be any that keep to these rules, and one draw needn't show every extreme that they name: `counts`: block 0 along the first dimension, 8 along the second is full; blocks near the injector hold several times the mean. `cells`: Non-decreasing along the slots of a block; slots that are not live hold 8191. `leave_slots`: entries below a face's count are live slots of that block, all distinct over the four faces; entries at or beyond the count are 0. `leave_counts`: some block sends 64 parcels through each of its faces.
All inputs are finite; a program needn't handle non-finite values.
Results may differ from a plain program's by a relative error of at most 0.0003.
Values sent between devices are 32-bit elements; how exact they have to be, the bound alone decides.
A program may use at most 32 MiB of HBM per device.

v0:
```python
import jax
import jax.numpy as jnp
from jax import lax
from jax.sharding import PartitionSpec as P

time_step = 0.1


def extended_2(x, sides, width):
    for axis, dim in sides:
        size, length = (lax.axis_size(axis), x.shape[dim])
        up = [(i, (i + 1) % size) for i in range(size - 1)]
        down = [(j, i) for i, j in up]
        last = lax.slice_in_dim(x, length - width, length, axis=dim)
        first = lax.slice_in_dim(x, 0, width, axis=dim)
        before = lax.ppermute(last, axis, up)
        after = lax.ppermute(first, axis, down)
        x = jnp.concatenate([before, x, after], axis=dim)
    return x


def coefficient(vel_first, vel_second, vel_third, base_rate):
    kinetic = vel_first * vel_first + vel_second * vel_second + vel_third * vel_third
    return base_rate * (1.0 + 0.5 * jnp.tanh(0.5 * kinetic))


def operate(values, diffusion):
    widths = [(0, 0)] * (values.ndim - 1) + [(1, 1)]
    padded = jnp.pad(values, widths)
    diffusion_padded = jnp.pad(diffusion, ((0, 0), (0, 0), (1, 1)))
    weight_first = 0.5 * (diffusion[1:] + diffusion[:-1])
    flux_first = weight_first * (values[..., 1:, :, :] - values[..., :-1, :, :])
    change_first = flux_first[..., 1:, :, :] - flux_first[..., :-1, :, :]
    weight_second = 0.5 * (diffusion[:, 1:] + diffusion[:, :-1])
    flux_second = weight_second * (values[..., :, 1:, :] - values[..., :, :-1, :])
    change_second = flux_second[..., :, 1:, :] - flux_second[..., :, :-1, :]
    weight_third = 0.5 * (diffusion_padded[:, :, 1:] + diffusion_padded[:, :, :-1])
    flux_third = weight_third * (padded[..., 1:] - padded[..., :-1])
    change_third = flux_third[..., 1:] - flux_third[..., :-1]
    return (
        change_first[..., :, 1:-1, :]
        + change_second[..., 1:-1, :, :]
        + change_third[..., 1:-1, 1:-1, :]
    )


def advance_parcels(parcel_block, live_count, cell_index, slot_table, face_counts, gas_flat):
    slots_total = parcel_block.shape[-1]
    movers = slot_table.shape[-1]
    gas_here = jnp.take(gas_flat, cell_index, axis=1)
    old_velocity = parcel_block[0:3]
    old_mass = parcel_block[3]
    response = parcel_block[4]
    evaporation = parcel_block[5]
    drag_force = response * (gas_here - old_velocity)
    new_velocity = old_velocity + time_step * drag_force
    new_mass = old_mass * (1.0 - time_step * evaporation)
    new_position = parcel_block[6:9] + time_step * new_velocity
    pushed = jnp.concatenate(
        [new_velocity, new_mass[None], parcel_block[4:6], new_position, parcel_block[9:]], axis=0
    )
    slot_ids = jnp.arange(slots_total, dtype=jnp.int32)
    live_weight = (slot_ids < live_count).astype(jnp.float32)
    deposits = (
        jnp.stack(
            [
                old_mass * evaporation,
                -old_mass * drag_force[0],
                -old_mass * drag_force[1],
                -old_mass * drag_force[2],
            ],
            axis=0,
        )
        * live_weight[None, :]
    )
    source = jnp.zeros((4, gas_flat.shape[1]), jnp.float32).at[:, cell_index].add(deposits)
    face_valid = (jnp.arange(movers, dtype=jnp.int32)[None, :] < face_counts[:, None]).astype(
        jnp.float32
    )
    leaving = (
        jnp.zeros((slots_total,), jnp.float32)
        .at[slot_table.reshape(-1)]
        .max(face_valid.reshape(-1))
    )
    staying = pushed * (live_weight * (1.0 - leaving))[None, :]
    outgoing = (
        jnp.transpose(jnp.take(pushed, slot_table, axis=1), (1, 0, 2)) * face_valid[:, None, :]
    )
    return (staying, outgoing, source)


def body(species, velocity, diffusivity, parcels, counts, cells, leave_slots, leave_counts):
    width_x = species.shape[1]
    width_y = species.shape[2]
    width_z = species.shape[3]
    gas_flat = velocity.reshape(3, width_x * width_y * width_z)
    staying, outgoing, source = advance_parcels(
        parcels[0, 0], counts[0, 0], cells[0, 0], leave_slots[0, 0], leave_counts[0, 0], gas_flat
    )
    source_grid = source.reshape(4, width_x, width_y, width_z)
    fields = jnp.concatenate([species, velocity, diffusivity[None]], axis=0)
    extended = extended_2(fields, (("axial", 1), ("radial", 2)), 2)
    base_cycle = extended[8, 1:-1, 1:-1]
    flow = extended[:8]
    start = coefficient(flow[5], flow[6], flow[7], extended[8])
    first = flow[:, 1:-1, 1:-1] + time_step * operate(flow, start)
    row_global = lax.axis_index("axial") * width_x - 1 + jnp.arange(width_x + 2, dtype=jnp.int32)
    column_global = (
        lax.axis_index("radial") * width_y - 1 + jnp.arange(width_y + 2, dtype=jnp.int32)
    )
    row_inside = (row_global >= 0) & (row_global < width_x * lax.axis_size("axial"))
    column_inside = (column_global >= 0) & (column_global < width_y * lax.axis_size("radial"))
    inside = row_inside[:, None] & column_inside[None, :]
    first = jnp.where(inside[None, :, :, None], first, 0.0)
    later = coefficient(first[5], first[6], first[7], base_cycle)
    second = 0.5 * (fields[:8] + first[:, 1:-1, 1:-1] + time_step * operate(first, later))
    zero_grid = jnp.zeros_like(source_grid[0])
    added = jnp.stack(
        [
            source_grid[0],
            zero_grid,
            zero_grid,
            zero_grid,
            zero_grid,
            source_grid[1],
            source_grid[2],
            source_grid[3],
        ],
        axis=0,
    )
    result = second + time_step * added
    axial_pair = jnp.stack([outgoing[1], outgoing[0]], axis=0)
    radial_pair = jnp.stack([outgoing[3], outgoing[2]], axis=0)
    axial_got = extended_2(axial_pair, (("axial", 0),), 1)
    radial_got = extended_2(radial_pair, (("radial", 0),), 1)
    arrivals = jnp.stack([axial_got[0], axial_got[3], radial_got[0], radial_got[3]], axis=0)
    return (result[:5], result[5:], staying[None, None], arrivals[None, None])


def solution(mesh):
    return jax.shard_map(
        body,
        mesh=mesh,
        in_specs=(
            P(None, "axial", "radial", None),
            P(None, "axial", "radial", None),
            P("axial", "radial", None),
            P("axial", "radial", None, None),
            P("axial", "radial"),
            P("axial", "radial", None),
            P("axial", "radial", None, None),
            P("axial", "radial", None),
        ),
        out_specs=(
            P(None, "axial", "radial", None),
            P(None, "axial", "radial", None),
            P("axial", "radial", None, None),
            P("axial", "radial", None, None, None),
        ),
        check_vma=False,
    )
```

profile of v0, /device:TPU:70, one launch (start us, length us, event | category | flops | bytes accessed | tf_op | source)
XLA Modules:
  0.0 123.5 jit_solution(16017610830809959467)
XLA Ops:
  0.6 1.5 %pad_maximum_fusion.8 = (f32[9,2,8,128]{3,2,1,0:T(8,128)}, f32[9,2,8,128]{3,2,1,0:T(8,128)}) fusion(f32[1,8,8,128]{3,2,1,0:T(8,128)} %bitcast.92, f32[3,8,8,128]{3,2,1,0:T(8,128)} %param.9, f32[5,8,8,128]{3,2,1,0:T(8,128)} %param.8), kind=kLoop, calls=%fused_computation.90 | loop fusion | flops 73728 | bytes 442368 | tf_op jit(solution)/shard_map/slice | solution.py:14
  2.2 1.9 %collective-permute-start = (f32[9,2,8,128]{3,2,1,0:T(8,128)}, f32[9,2,8,128]{3,2,1,0:T(8,128)S(1)}, u32[]{:S(2)}, u32[]{:S(2)}) collective-permute-start(f32[9,2,8,128]{3,2,1,0:T(8,128)} %get-tuple-element.35), channel_id=1, source_target_pairs={{0,16},{16,32},{32,48},{48,64},{64,80},{80,96},{96,112},{112,128},... | collective-permute-start | bytes 221192 | tf_op jit(solution)/shard_map/ppermute | solution.py:16
  4.1 5.9 %collective-permute-start.1 = (f32[9,2,8,128]{3,2,1,0:T(8,128)}, f32[9,2,8,128]{3,2,1,0:T(8,128)S(1)}, u32[]{:S(2)}, u32[]{:S(2)}) collective-permute-start(f32[9,2,8,128]{3,2,1,0:T(8,128)} %get-tuple-element.36), channel_id=1, source_target_pairs={{16,0},{32,16},{48,32},{64,48},{80,64},{96,80},{112,96},{128,112},... | collective-permute-start | bytes 221192 | tf_op jit(solution)/shard_map/ppermute | solution.py:17
  10.0 3.4 %copy.76 = f32[3,8,8,128]{0,3,2,1:T(8,128)} copy(f32[3,8,8,128]{3,2,1,0:T(8,128)} %param.9) | data formatting | bytes 196608 | tf_op args[1]
  13.5 0.6 copy-done.5
  14.1 7.6 %gather_fusion = f32[2048,3]{1,0:T(8,128)S(1)} fusion(f32[3,8192]{0,1:T(8,128)} %bitcast.87, s32[2048]{0:T(1024)S(1)} %broadcast_clamp_fusion), kind=kCustom, calls=%fused_computation | custom fusion | bytes 57344 | tf_op jit(solution)/shard_map/jit(_take)/gather | solution.py:50
  21.7 0.3 copy.77
  22.1 0.7 bitcast_add_fusion
  22.8 0.7 fusion.52
  23.4 0.4 copy.85
  23.8 0.4 copy.84
  24.1 1.1 copy.86
  25.3 1.4 %copy.89 = f32[1,1,7,2048]{2,3,1,0:T(8,128)} copy(f32[1,1,7,2048]{3,2,1,0:T(8,128)S(1)} %slice.345) | data formatting | bytes 114688
  26.7 1.3 %copy.88 = f32[1,1,2,2048]{2,3,1,0:T(8,128)} copy(f32[1,1,2,2048]{3,2,1,0:T(2,128)S(1)} %slice.343) | data formatting | bytes 32768
  28.0 1.3 %compare_select_fusion.3 = s32[4,64,1]{1,0,2:T(4,128)} fusion(s32[1,1,4,64]{3,2,1,0:T(4,128)} %param.14), kind=kLoop, calls=%fused_computation.128 | loop fusion | flops 768 | bytes 2048 | tf_op jit(solution)/shard_map/jit(_take)/jit(_where)/select_n | solution.py:87
  29.3 1.3 %reshape.414 = s32[256]{0:T(256)} reshape(s32[4,64,1]{1,0,2:T(4,128)} %compare_select_fusion.3) | data formatting | bytes 2048 | tf_op jit(solution)/shard_map/jit(_take)/jit(_where)/select_n | solution.py:87
  30.6 1.2 pad_clamp_fusion
  31.8 4.3 %concatenate.29 = f32[16,2048]{0,1:T(8,128)} concatenate(f32[3,2048]{0,1:T(8,128)S(1)} %copy.84, f32[1,2048]{0,1:T(8,128)S(1)} %copy.85, f32[2,2048]{0,1:T(8,128)} %bitcast.89, f32[3,2048]{0,1:T(8,128)S(1)} %copy.86, f32[7,2048]{0,1:T(8,128)} %bitcast.88), dimensions={0} | concatenate | bytes 262144 | tf_op jit(solution)/shard_map/concatenate | solution.py:59
  36.1 2.1 %gather_fusion.1 = f32[256,16]{1,0:T(8,128)S(1)} fusion(f32[16,2048]{0,1:T(8,128)} %concatenate.29, s32[1024]{0:T(1024)} %pad_clamp_fusion), kind=kCustom, calls=%fused_computation.1 | custom fusion | bytes 33792 | tf_op jit(solution)/shard_map/jit(_take)/gather | solution.py:87
  38.2 0.8 fusion.56
  39.0 1.9 %collective-permute-start.4 = (f32[1,16,64]{2,1,0:T(8,128)S(1)}, f32[1,16,64]{2,1,0:T(8,128)S(1)}, u32[]{:S(2)}, u32[]{:S(2)}) collective-permute-start(f32[1,16,64]{2,1,0:T(8,128)S(1)} %get-tuple-element.47), channel_id=1, source_target_pairs={{0,16},{16,32},{32,48},{48,64},{64,80},{80,96},{96,112},{112,128},... | collective-permute-start | bytes 12296 | tf_op jit(solution)/shard_map/ppermute | solution.py:16
  40.9 5.8 %collective-permute-start.5 = (f32[1,16,64]{2,1,0:T(8,128)S(1)}, f32[1,16,64]{2,1,0:T(8,128)S(1)}, u32[]{:S(2)}, u32[]{:S(2)}) collective-permute-start(f32[1,16,64]{2,1,0:T(8,128)S(1)} %get-tuple-element.50), channel_id=1, source_target_pairs={{16,0},{32,16},{48,32},{64,48},{80,64},{96,80},{112,96},{128,112},... | collective-permute-start | bytes 12296 | tf_op jit(solution)/shard_map/ppermute | solution.py:17
  46.7 11.4 %collective-permute-start.6 = (f32[1,16,64]{2,1,0:T(8,128)S(1)}, f32[1,16,64]{2,1,0:T(8,128)S(1)}, u32[]{:S(2)}, u32[]{:S(2)}) collective-permute-start(f32[1,16,64]{2,1,0:T(8,128)S(1)} %get-tuple-element.49), channel_id=1, source_target_pairs={{0,1},{1,2},{2,3},{3,4},{4,5},{5,6},{6,7},{7,8},{8,9},{9,10},{10,1... | collective-permute-start | bytes 12296 | tf_op jit(solution)/shard_map/ppermute | solution.py:16
  58.2 0.7 multiply_add_fusion
  59.0 0.8 reshape_squeeze.3
  60.4 0.8 fusion.45
  61.2 0.4 copy.78
  61.5 16.3 %scatter_custom_fusion = f32[4,8192]{0,1:T(8,128)} fusion(s32[2048]{0:T(1024)} %bitcast.100, f32[2048,4]{1,0:T(8,128)S(1)} %copy.78, f32[]{:T(128)} %constant.28.clone.1), kind=kCustom, calls=%fused_computation.8 | custom fusion | flops 8192 | bytes 131584 | tf_op jit(solution)/shard_map/scatter-add | solution.py:76
  77.8 13.9 %slice_reduce_fusion = (f32[8192]{0:T(1024)S(1)}, f32[8192]{0:T(1024)S(1)}, f32[8192]{0:T(1024)S(1)}, f32[8192]{0:T(1024)S(1)}) fusion(f32[4,8192]{0,1:T(8,128)} %scatter_custom_fusion), kind=kLoop, calls=%fused_computation.4 | loop fusion | bytes 262144 | tf_op jit(solution)/shard_map/slice | solution.py:127
  91.8 2.3 %scatter_custom_fusion.1 = f32[2048]{0:T(1024)S(1)} fusion(s32[256]{0:T(256)S(1)} %bitcast.101, f32[256]{0:T(256)S(1)} %reshape.432, f32[]{:T(128)} %constant.28.clone.1), kind=kCustom, calls=%fused_computation.132 | custom fusion | flops 256 | bytes 8196 | tf_op jit(solution)/shard_map/scatter-max | solution.py:83
  94.2 0.2 concatenate.28
  94.4 0.7 broadcast_multiply_fusion
  95.2 1.9 %collective-permute-start.7 = (f32[1,16,64]{2,1,0:T(8,128)S(1)}, f32[1,16,64]{2,1,0:T(8,128)S(1)}, u32[]{:S(2)}, u32[]{:S(2)}) collective-permute-start(f32[1,16,64]{2,1,0:T(8,128)S(1)} %get-tuple-element.48), channel_id=1, source_target_pairs={{1,0},{2,1},{3,2},{4,3},{5,4},{6,5},{7,6},{8,7},{9,8},{10,9},{11,1... | collective-permute-start | bytes 12296 | tf_op jit(solution)/shard_map/ppermute | solution.py:17
  97.2 9.0 %collective-permute-start.2 = (f32[9,12,2,128]{3,2,1,0:T(2,128)S(1)}, f32[9,12,2,128]{3,2,1,0:T(2,128)S(1)}, u32[]{:S(2)}, u32[]{:S(2)}) collective-permute-start(f32[9,12,2,128]{3,2,1,0:T(2,128)S(1)} %get-tuple-element.33), channel_id=1, source_target_pairs={{0,1},{1,2},{2,3},{3,4},{4,5},{5,6},{6,7},{7,8},{8,9},{9,10},{10,1... | collective-permute-start | bytes 331784 | tf_op jit(solution)/shard_map/ppermute | solution.py:16
  106.3 2.1 %collective-permute-start.3 = (f32[9,12,2,128]{3,2,1,0:T(2,128)S(1)}, f32[9,12,2,128]{3,2,1,0:T(2,128)S(1)}, u32[]{:S(2)}, u32[]{:S(2)}) collective-permute-start(f32[9,12,2,128]{3,2,1,0:T(2,128)S(1)} %get-tuple-element.34), channel_id=1, source_target_pairs={{1,0},{2,1},{3,2},{4,3},{5,4},{6,5},{7,6},{8,7},{9,8},{10,9},{11,1... | collective-permute-start | bytes 331784 | tf_op jit(solution)/shard_map/ppermute | solution.py:17
  108.4 0.6 maximum_bitcast_fusion
  109.0 9.6 %collective-permute-done.3 = f32[9,12,2,128]{3,2,1,0:T(2,128)S(1)} collective-permute-done((f32[9,12,2,128]{3,2,1,0:T(2,128)S(1)}, f32[9,12,2,128]{3,2,1,0:T(2,128)S(1)}, u32[]{:S(2)}, u32[]{:S(2)}) %collective-permute-start.3) | collective-permute-done | bytes 110624 | tf_op jit(solution)/shard_map/ppermute | solution.py:17
  118.7 0.2 pad_maximum_fusion
  119.1 0.5 fusion.3
  119.6 0.3 fusion.59
  119.9 0.1 fusion.6
  120.0 0.1 fusion.61
  120.4 0.4 fusion.12
  121.3 0.4 fusion.5
  121.7 0.2 fusion.60
  122.0 0.3 fusion.19
  122.2 0.7 slice.419
  122.9 0.6 slice.420
  (57 shorter events, 1.4 us)
Async XLA Ops:
  2.2 93.0 %collective-permute-start = (f32[9,2,8,128]{3,2,1,0:T(8,128)}, f32[9,2,8,128]{3,2,1,0:T(8,128)S(1)}, u32[]{:S(2)}, u32[]{:S(2)}) collective-permute-start(f32[9,2,8,128]{3,2,1,0:T(8,128)} %get-tuple-element.35), channel_id=1, source_target_pairs={{0,16},{16,32},{32,48},{48,64},{64,80},{80,96},{96,112},{112,128},... | collective-permute-start | bytes 221192 | tf_op jit(solution)/shard_map/ppermute | solution.py:16
  4.1 9.3 %copy-start.2 = (f32[1,1,16,2048]{3,2,1,0:T(8,128)S(1)}, f32[1,1,16,2048]{3,2,1,0:T(8,128)}, u32[]{:S(2)}) copy-start(f32[1,1,16,2048]{3,2,1,0:T(8,128)} %param.11) | copy-start | bytes 393220
  4.1 9.4 %copy-start.4 = (s32[1,1,2048]{2,1,0:T(1,128)S(1)}, s32[1,1,2048]{2,1,0:T(1,128)}, u32[]{:S(2)}) copy-start(s32[1,1,2048]{2,1,0:T(1,128)} %param.13) | copy-start | bytes 24580
  4.1 93.0 %collective-permute-start.1 = (f32[9,2,8,128]{3,2,1,0:T(8,128)}, f32[9,2,8,128]{3,2,1,0:T(8,128)S(1)}, u32[]{:S(2)}, u32[]{:S(2)}) collective-permute-start(f32[9,2,8,128]{3,2,1,0:T(8,128)} %get-tuple-element.36), channel_id=1, source_target_pairs={{16,0},{32,16},{48,32},{64,48},{80,64},{96,80},{112,96},{128,112},... | collective-permute-start | bytes 221192 | tf_op jit(solution)/shard_map/ppermute | solution.py:17
  13.5 0.6 copy-start.5
  22.1 0.7 copy-start.6
  39.0 67.2 %collective-permute-start.4 = (f32[1,16,64]{2,1,0:T(8,128)S(1)}, f32[1,16,64]{2,1,0:T(8,128)S(1)}, u32[]{:S(2)}, u32[]{:S(2)}) collective-permute-start(f32[1,16,64]{2,1,0:T(8,128)S(1)} %get-tuple-element.47), channel_id=1, source_target_pairs={{0,16},{16,32},{32,48},{48,64},{64,80},{80,96},{96,112},{112,128},... | collective-permute-start | bytes 12296 | tf_op jit(solution)/shard_map/ppermute | solution.py:16
  40.9 67.4 %collective-permute-start.5 = (f32[1,16,64]{2,1,0:T(8,128)S(1)}, f32[1,16,64]{2,1,0:T(8,128)S(1)}, u32[]{:S(2)}, u32[]{:S(2)}) collective-permute-start(f32[1,16,64]{2,1,0:T(8,128)S(1)} %get-tuple-element.50), channel_id=1, source_target_pairs={{16,0},{32,16},{48,32},{64,48},{80,64},{96,80},{112,96},{128,112},... | collective-permute-start | bytes 12296 | tf_op jit(solution)/shard_map/ppermute | solution.py:17
  46.7 61.7 %collective-permute-start.6 = (f32[1,16,64]{2,1,0:T(8,128)S(1)}, f32[1,16,64]{2,1,0:T(8,128)S(1)}, u32[]{:S(2)}, u32[]{:S(2)}) collective-permute-start(f32[1,16,64]{2,1,0:T(8,128)S(1)} %get-tuple-element.49), channel_id=1, source_target_pairs={{0,1},{1,2},{2,3},{3,4},{4,5},{5,6},{6,7},{7,8},{8,9},{9,10},{10,1... | collective-permute-start | bytes 12296 | tf_op jit(solution)/shard_map/ppermute | solution.py:16
  77.8 19.3 %copy-start = (f32[5,8,8,128]{3,2,1,0:T(8,128)S(1)}, f32[5,8,8,128]{3,2,1,0:T(8,128)}, u32[]{:S(2)}) copy-start(f32[5,8,8,128]{3,2,1,0:T(8,128)} %param.8) | copy-start | bytes 491524
  77.8 19.3 %copy-start.1 = (f32[3,8,8,128]{3,2,1,0:T(8,128)S(1)}, f32[3,8,8,128]{3,2,1,0:T(8,128)}, u32[]{:S(2)}) copy-start(f32[3,8,8,128]{3,2,1,0:T(8,128)} %param.9) | copy-start | bytes 294916
  77.8 19.3 %copy-start.3 = (f32[8,8,128]{2,1,0:T(8,128)S(1)}, f32[8,8,128]{2,1,0:T(8,128)}, u32[]{:S(2)}) copy-start(f32[8,8,128]{2,1,0:T(8,128)} %param.10) | copy-start | bytes 98308
  95.2 13.2 %collective-permute-start.7 = (f32[1,16,64]{2,1,0:T(8,128)S(1)}, f32[1,16,64]{2,1,0:T(8,128)S(1)}, u32[]{:S(2)}, u32[]{:S(2)}) collective-permute-start(f32[1,16,64]{2,1,0:T(8,128)S(1)} %get-tuple-element.48), channel_id=1, source_target_pairs={{1,0},{2,1},{3,2},{4,3},{5,4},{6,5},{7,6},{8,7},{9,8},{10,9},{11,1... | collective-permute-start | bytes 12296 | tf_op jit(solution)/shard_map/ppermute | solution.py:17
  97.2 11.8 %collective-permute-start.2 = (f32[9,12,2,128]{3,2,1,0:T(2,128)S(1)}, f32[9,12,2,128]{3,2,1,0:T(2,128)S(1)}, u32[]{:S(2)}, u32[]{:S(2)}) collective-permute-start(f32[9,12,2,128]{3,2,1,0:T(2,128)S(1)} %get-tuple-element.33), channel_id=1, source_target_pairs={{0,1},{1,2},{2,3},{3,4},{4,5},{5,6},{6,7},{7,8},{8,9},{9,10},{10,1... | collective-permute-start | bytes 331784 | tf_op jit(solution)/shard_map/ppermute | solution.py:16
  106.3 12.4 %collective-permute-start.3 = (f32[9,12,2,128]{3,2,1,0:T(2,128)S(1)}, f32[9,12,2,128]{3,2,1,0:T(2,128)S(1)}, u32[]{:S(2)}, u32[]{:S(2)}) collective-permute-start(f32[9,12,2,128]{3,2,1,0:T(2,128)S(1)} %get-tuple-element.34), channel_id=1, source_target_pairs={{1,0},{2,1},{3,2},{4,3},{5,4},{6,5},{7,6},{8,7},{9,8},{10,9},{11,1... | collective-permute-start | bytes 331784 | tf_op jit(solution)/shard_map/ppermute | solution.py:17
where the time goes:
time: 124 us
  local copies, waits for them, and re-layouts  41.9 us (34%)
  starting transfers between devices  40 us (32%)
  other arithmetic  30.2 us (24%)
  waiting for transfers between devices  9.66 us (8%)
  between operations  1.83 us (1%)
    ppermute x4, starting transfers between devices, extended_2(): before = lax.ppermute(last, axis, up)  24.3 us
    scatter-add x1, other arithmetic, advance_parcels(): jnp.zeros((4, gas_flat.shape[1]), jnp.float32).at[:, cell_index]  16.3 us
    ppermute x4, starting transfers between devices, extended_2(): after = lax.ppermute(first, axis, down)  15.6 us
    slice x1, local copies, waits for them, and re-layouts, body(): source_grid[3]  13.9 us
    ppermute x4, waiting for transfers between devices, extended_2(): after = lax.ppermute(first, axis, down)  9.65 us
    gather x2, local copies, waits for them, and re-layouts, advance_parcels(): gas_here = jnp.take(gas_flat, cell_index, axis=1)  7.98 us
    unnamed x21, local copies, waits for them, and re-layouts  6.76 us
    concatenate x2, local copies, waits for them, and re-layouts, advance_parcels(): jnp.concatenate([new_velocity, new_mass[None], parcel_block[4:6], new_pos...  4.46 us
  transfers between devices with their start and end apart: 8, of which 1 were waited for; matrix products, arithmetic and copies ran while one was open for 53% of the time, Pallas kernels for 0%

commit v1 on v0

v1 whole, which is shorter than its diff:
```python
import functools

import jax
import jax.numpy as jnp
from jax import lax
from jax.experimental import pallas as pl
from jax.experimental.pallas import tpu as pltpu
from jax.sharding import PartitionSpec as P

MESH = pl.DeviceIdType.MESH
F32, BF16, I32 = jnp.float32, jnp.bfloat16, jnp.int32
time_step = 0.1
CHUNK = 512
STEPS = ((0, 1), (0, -1), (1, 0), (-1, 0), (1, 1), (1, -1), (-1, 1), (-1, -1))
FACES = ((1, 0), (-1, 0), (0, 1), (0, -1))


def ranges(step, depth):
    if step == 0:
        return (2, 8), (2, 8)
    if step > 0:
        return (10 - depth, depth), (2 - depth, depth)
    return (2, depth), (10, depth)


def coefficient(values, base):
    row = lax.broadcasted_iota(I32, (8, 128), 0)
    kinetic = jnp.where(row >= 5, values * values, 0.0)
    for shift in (4, 2, 1):
        kinetic = kinetic + pltpu.roll(kinetic, shift, 0)
    return base * (1.0 + 0.5 * jnp.tanh(0.5 * kinetic))


def pieces(x):
    high = x.astype(BF16)
    rest = x - high.astype(F32)
    middle = rest.astype(BF16)
    low = (rest - middle.astype(F32)).astype(BF16)
    return high, middle, low


def one_hot(rows, index):
    row = lax.broadcasted_iota(I32, (rows, index.shape[1]), 0)
    return jnp.where(row == index, 1.0, 0.0).astype(BF16)


def dot_nt(a, b):
    return lax.dot_general(a, b, (((1,), (1,)), ((), ())), preferred_element_type=F32)


def exchange_kernel(
    n_a, n_r, species, velocity, diffusivity, parcels, counts, cells, slots, faces,
    ext, base, start, source, staying, arrivals,
    vel, par, cnt, cel, slo, fac, vel3, pushed, leaving, outgoing,
    load_sem, send_sem, recv_sem, base_send, base_recv, row_send, row_recv,
):
    a, r = lax.axis_index("axial"), lax.axis_index("radial")

    def there(step_a, step_r):
        ok = None
        for step, at, size in ((step_a, a, n_a), (step_r, r, n_r)):
            if step:
                here = at < size - 1 if step > 0 else at > 0
                ok = here if ok is None else jnp.logical_and(ok, here)
        return ok

    barrier = pltpu.get_barrier_semaphore()
    total = jnp.int32(0)
    for da, dr in STEPS:
        ok = there(da, dr)
        total = total + ok.astype(I32)

        @pl.when(ok)
        def _(da=da, dr=dr):
            pl.semaphore_signal(barrier, inc=1, device_id=(a + da, r + dr), device_id_type=MESH)

    loads = [pltpu.make_async_copy(species.at[f], ext.at[2:10, 2:10, f], load_sem.at[f]) for f in range(5)]
    loads += [pltpu.make_async_copy(velocity.at[k], ext.at[2:10, 2:10, 5 + k], load_sem.at[5 + k]) for k in range(3)]
    loads.append(pltpu.make_async_copy(diffusivity, base.at[2:10, 2:10, 0], load_sem.at[8]))
    own_loads = len(loads)
    for k, (src, dst) in enumerate(
        ((velocity, vel), (parcels, par), (counts, cnt), (cells, cel), (slots, slo), (faces, fac))
    ):
        loads.append(pltpu.make_async_copy(src, dst, load_sem.at[9 + k]))
    for load in loads:
        load.start()

    zero2 = jnp.zeros((2, 8, 8, 128), F32)
    zero3 = jnp.zeros((8, 2, 8, 128), F32)
    corner = jnp.zeros((8, 128), F32)

    def clear_corner(x, y):
        ext[x, y] = corner
        base[x, y] = corner[:1]

    @pl.when(a == 0)
    def _():
        ext[0:2, 2:10] = zero2
        base[0:2, 2:10] = zero2[:, :, :1]
        arrivals[0] = jnp.zeros((16, 64), F32)
        clear_corner(1, 1)
        clear_corner(1, 10)

    @pl.when(a == n_a - 1)
    def _():
        ext[10:12, 2:10] = zero2
        base[10:12, 2:10] = zero2[:, :, :1]
        arrivals[1] = jnp.zeros((16, 64), F32)
        clear_corner(10, 1)
        clear_corner(10, 10)

    @pl.when(r == 0)
    def _():
        ext[2:10, 0:2] = zero3
        base[2:10, 0:2] = zero3[:, :, :1]
        arrivals[2] = jnp.zeros((16, 64), F32)
        clear_corner(1, 1)
        clear_corner(10, 1)

    @pl.when(r == n_r - 1)
    def _():
        ext[2:10, 10:12] = zero3
        base[2:10, 10:12] = zero3[:, :, :1]
        arrivals[3] = jnp.zeros((16, 64), F32)
        clear_corner(1, 10)
        clear_corner(10, 10)

    for load in loads[:own_loads]:
        load.wait()
    pl.semaphore_wait(barrier, total)

    def halo(k):
        da, dr = STEPS[k]
        depth = 1 if da and dr else 2
        (sx, nx), (tx, _) = ranges(da, depth)
        (sy, ny), (ty, _) = ranges(dr, depth)
        device = (a + da, r + dr)
        return (
            pltpu.make_async_remote_copy(
                src_ref=ext.at[sx : sx + nx, sy : sy + ny],
                dst_ref=ext.at[tx : tx + nx, ty : ty + ny],
                send_sem=send_sem.at[k], recv_sem=recv_sem.at[k],
                device_id=device, device_id_type=MESH,
            ),
            pltpu.make_async_remote_copy(
                src_ref=base.at[sx : sx + nx, sy : sy + ny],
                dst_ref=base.at[tx : tx + nx, ty : ty + ny],
                send_sem=base_send.at[k], recv_sem=base_recv.at[k],
                device_id=device, device_id_type=MESH,
            ),
        )

    for k, (da, dr) in enumerate(STEPS):

        @pl.when(there(da, dr))
        def _(k=k):
            for copy in halo(k):
                copy.start()

    for load in loads[own_loads:]:
        load.wait()

    leave_sum = jnp.zeros((16, 128), F32)
    low_hot, high_row = [], []
    for f in range(4):
        member = lax.broadcasted_iota(I32, (1, 64), 1)
        slot = jnp.where(member < fac[0:1, f : f + 1], slo[f : f + 1, :], -1)
        high_row.append(slot >> 7)
        low_hot.append(one_hot(128, slot & 127))
        leave_sum = leave_sum + dot_nt(one_hot(16, slot >> 7), low_hot[f])
    leaving[...] = leave_sum

    vel3[...] = jnp.concatenate(pieces(vel[...].reshape(192, 128)), axis=1)
    source[...] = jnp.zeros((512, 128), F32)

    def parcel_step(c, _):
        span = pl.ds(pl.multiple_of(c * CHUNK, CHUNK), CHUNK)
        cell = cel[:, span]
        plane, depth = cell >> 7, cell & 127
        depth_hot = one_hot(128, depth)
        rows = jnp.dot(vel3[...], jnp.concatenate([depth_hot] * 3, axis=0), preferred_element_type=F32)
        here = lax.broadcasted_iota(I32, (64, CHUNK), 0) == plane
        gas = jnp.concatenate(
            [
                jnp.sum(jnp.where(here, rows[64 * k : 64 * k + 64], 0.0), axis=0, keepdims=True)
                for k in range(3)
            ],
            axis=0,
        )
        old = par[:, span]
        mass, evaporation = old[3:4], old[5:6]
        drag = old[4:5] * (gas - old[0:3])
        new_velocity = old[0:3] + time_step * drag
        pushed[:, span] = old
        pushed[0:3, span] = new_velocity
        pushed[3:4, span] = mass * (1.0 - time_step * evaporation)
        pushed[6:9, span] = old[6:9] + time_step * new_velocity
        live = lax.broadcasted_iota(I32, (1, CHUNK), 1) + c * CHUNK < cnt[0:1, 0:1]
        leave = jnp.concatenate(
            [leaving[pl.ds(c * (CHUNK // 128) + j, 1), :] for j in range(CHUNK // 128)], axis=1
        )
        keep = jnp.logical_and(live, leave == 0.0)
        staying[:, span] = jnp.where(keep, pushed[:, span], 0.0)
        deposit = [mass * evaporation] + [-mass * drag[k : k + 1] for k in range(3)]
        split = [pieces(jnp.where(live, d, 0.0)) for d in deposit]
        added = jnp.zeros((256, 128), F32)
        for p in range(3):
            spread = jnp.concatenate(
                [jnp.where(here, split[k][p].astype(F32), 0.0).astype(BF16) for k in range(4)], axis=0
            )
            added = added + dot_nt(spread, depth_hot)
        source[0:64] += added[0:64]
        source[320:512] += added[64:256]
        return 0

    lax.fori_loop(0, 2048 // CHUNK, parcel_step, 0)

    stacked = jnp.concatenate([pushed[:, 128 * h : 128 * h + 128] for h in range(16)], axis=0)
    stacked3 = jnp.concatenate(pieces(stacked), axis=1)
    for f in range(4):
        picked = jnp.dot(stacked3, jnp.concatenate([low_hot[f]] * 3, axis=0), preferred_element_type=F32)
        out = jnp.zeros((16, 64), F32)
        for h in range(16):
            out = out + jnp.where(high_row[f] == h, picked[16 * h : 16 * h + 16], 0.0)
        outgoing[f] = out

    def own_start(x, _):
        for y in range(2, 10):
            start[x, y] = coefficient(ext[x, y], base[x, y])
        return 0

    lax.fori_loop(2, 10, own_start, 0)

    def row_copy(f):
        da, dr = FACES[f]
        return pltpu.make_async_remote_copy(
            src_ref=outgoing.at[f], dst_ref=arrivals.at[f],
            send_sem=row_send.at[f], recv_sem=row_recv.at[f],
            device_id=(a + da, r + dr), device_id_type=MESH,
        )

    for f in (2, 3, 0, 1):

        @pl.when(there(*FACES[f]))
        def _(f=f):
            row_copy(f).start()

    for k, (da, dr) in enumerate(STEPS):

        @pl.when(there(-da, -dr))
        def _(k=k):
            for copy in halo(k):
                copy.wait_recv()

    for f, (da, dr) in enumerate(FACES):

        @pl.when(there(-da, -dr))
        def _(f=f):
            row_copy(f).wait_recv()

    for k, (da, dr) in enumerate(STEPS):

        @pl.when(there(da, dr))
        def _(k=k):
            for copy in halo(k):
                copy.wait_send()

    for f, (da, dr) in enumerate(FACES):

        @pl.when(there(da, dr))
        def _(f=f):
            row_copy(f).wait_send()


def z_up(x):
    lane = lax.broadcasted_iota(I32, (8, 128), 1)
    return jnp.where(lane == 127, 0.0, pltpu.roll(x, 127, 1))


def change(value, coef, below, below_coef, above, above_coef, flux_y):
    lane = lax.broadcasted_iota(I32, (8, 128), 1)
    flux_x = (coef + above_coef) * (above - value) - (below_coef + coef) * (value - below)
    up = (coef + z_up(coef)) * (z_up(value) - value)
    down = jnp.where(lane == 0, coef * value, pltpu.roll(up, 1, 1))
    return flux_x + flux_y + (up - down)


def stencil_kernel(
    n_a, n_r, ext, base, own_start, source, staying, arrivals,
    species_out, velocity_out, staying_out, arrivals_out,
    start, first, later, result, sems,
):
    a, r = lax.axis_index("axial"), lax.axis_index("radial")
    early = [
        pltpu.make_async_copy(staying, staying_out, sems.at[0]),
        pltpu.make_async_copy(arrivals, arrivals_out, sems.at[1]),
    ]
    for copy in early:
        copy.start()

    def copy_start(x, _):
        for y in range(2, 10):
            start[x, y] = own_start[x, y]
        for y in (0, 1, 10, 11):
            start[x, y] = coefficient(ext[x, y], base[x, y])
        return 0

    lax.fori_loop(2, 10, copy_start, 0)
    for x in (0, 11):
        for y in range(2, 10):
            start[x, y] = coefficient(ext[x, y], base[x, y])
    for x in (1, 10):
        for y in range(1, 11):
            start[x, y] = coefficient(ext[x, y], base[x, y])

    def first_row(x, low, high, outside):
        values = {y: ext[x, y] for y in range(low - 1, high + 1)}
        coefs = {y: start[x, y] for y in range(low - 1, high + 1)}
        fluxes = {y: (coefs[y] + coefs[y + 1]) * (values[y + 1] - values[y]) for y in range(low - 1, high)}
        for y in range(low, high):
            twice = change(
                values[y], coefs[y], ext[x - 1, y], start[x - 1, y], ext[x + 1, y], start[x + 1, y],
                fluxes[y] - fluxes[y - 1],
            )
            new = values[y] + (0.5 * time_step) * twice
            zero = outside
            if y == 1:
                zero = r == 0
            if y == 10:
                zero = r == n_r - 1
            if zero is not None:
                new = jnp.where(zero, 0.0, new)
            first[x, y] = new
            later[x, y] = coefficient(new, base[x, y])

    def inner_row(x, _):
        first_row(x, 1, 11, None)
        return 0

    first_row(1, 2, 10, a == 0)
    first_row(10, 2, 10, a == n_a - 1)
    lax.fori_loop(2, 10, inner_row, 0)

    def second_row(x, _):
        values = {y: first[x, y] for y in range(1, 11)}
        coefs = {y: later[x, y] for y in range(1, 11)}
        fluxes = {y: (coefs[y] + coefs[y + 1]) * (values[y + 1] - values[y]) for y in range(1, 10)}
        for y in range(2, 10):
            twice = change(
                values[y], coefs[y], first[x - 1, y], later[x - 1, y], first[x + 1, y], later[x + 1, y],
                fluxes[y] - fluxes[y - 1],
            )
            cell = (x - 2) * 8 + (y - 2)
            added = source[pl.ds(cell, 8, stride=64), :]
            result[pl.ds(cell, 8, stride=64), :] = (
                0.5 * (ext[x, y] + values[y]) + (0.25 * time_step) * twice + time_step * added
            )
        return 0

    lax.fori_loop(2, 10, second_row, 0)
    last = [
        pltpu.make_async_copy(result.at[0:320], species_out, sems.at[2]),
        pltpu.make_async_copy(result.at[320:512], velocity_out, sems.at[3]),
    ]
    for copy in last:
        copy.start()
    for copy in early + last:
        copy.wait()


def body(n_a, n_r, species, velocity, diffusivity, parcels, counts, cells, leave_slots, leave_counts):
    anywhere = pl.BlockSpec(memory_space=pl.ANY)
    vmem = pl.BlockSpec(memory_space=pltpu.VMEM)
    shape = lambda *dims: jax.ShapeDtypeStruct(dims, F32)
    local = lambda *dims: pltpu.VMEM(dims, F32)
    dma = pltpu.SemaphoreType.DMA
    between = pl.pallas_call(
        functools.partial(exchange_kernel, n_a, n_r),
        name="exchange",
        out_shape=[
            local(12, 12, 8, 128), local(12, 12, 1, 128), local(12, 12, 8, 128), local(512, 128),
            local(16, 2048), local(4, 16, 64),
        ],
        in_specs=[anywhere] * 4 + [pl.BlockSpec(memory_space=pltpu.HBM)] + [anywhere] * 3,
        out_specs=[vmem] * 6,
        scratch_shapes=[
            pltpu.VMEM((3, 8, 8, 128), F32), pltpu.VMEM((16, 2048), F32), pltpu.VMEM((1, 1), I32),
            pltpu.VMEM((1, 2048), I32), pltpu.VMEM((4, 64), I32), pltpu.VMEM((1, 4), I32),
            pltpu.VMEM((192, 384), BF16), pltpu.VMEM((16, 2048), F32), pltpu.VMEM((16, 128), F32),
            pltpu.VMEM((4, 16, 64), F32),
            dma((15,)), dma((8,)), dma((8,)), dma((8,)), dma((8,)), dma((4,)), dma((4,)),
        ],
        compiler_params=pltpu.CompilerParams(collective_id=0, has_side_effects=True),
    )(
        species, velocity, diffusivity, parcels[0, 0], counts, cells[0], leave_slots[0, 0], leave_counts[0],
    )
    species_out, velocity_out, staying, arrivals = pl.pallas_call(
        functools.partial(stencil_kernel, n_a, n_r),
        name="stencil",
        out_shape=[shape(320, 128), shape(192, 128), shape(16, 2048), shape(4, 16, 64)],
        in_specs=[vmem] * 6,
        out_specs=[anywhere] * 4,
        scratch_shapes=[
            pltpu.VMEM((12, 12, 8, 128), F32), pltpu.VMEM((12, 12, 8, 128), F32),
            pltpu.VMEM((12, 12, 8, 128), F32), pltpu.VMEM((512, 128), F32), dma((4,)),
        ],
    )(*[pltpu.with_memory_space_constraint(x, pltpu.VMEM) for x in between])
    return (
        species_out.reshape(5, 8, 8, 128), velocity_out.reshape(3, 8, 8, 128),
        staying[None, None], arrivals[None, None],
    )


def solution(mesh):
    return jax.shard_map(
        functools.partial(body, mesh.shape["axial"], mesh.shape["radial"]),
        mesh=mesh,
        in_specs=(
            P(None, "axial", "radial", None),
            P(None, "axial", "radial", None),
            P("axial", "radial", None),
            P("axial", "radial", None, None),
            P("axial", "radial"),
            P("axial", "radial", None),
            P("axial", "radial", None, None),
            P("axial", "radial", None),
        ),
        out_specs=(
            P(None, "axial", "radial", None),
            P(None, "axial", "radial", None),
            P("axial", "radial", None, None),
            P("axial", "radial", None, None, None),
        ),
        check_vma=False,
    )
```

time: 124 us -> 24.6 us (0.20)
  the two profiles are of different devices: /device:TPU:70 before, /device:TPU:255 now
where the time goes in v1:
time: 24.6 us; the launch traced here: 24.5 us
  Pallas kernels  23.2 us (94%)
  between operations  1.29 us (5%)
    pallas_call x1, Pallas kernels, body(): pl.pallas_call(functools.partial(exchange_kernel, n_a, n_r), name='exchan...  19.3 us
    pallas_call x1, Pallas kernels, body(): pl.pallas_call(functools.partial(stencil_kernel, n_a, n_r), name='stencil...  3.94 us

profile of v1, /device:TPU:255, one launch (start us, length us, event | category | flops | bytes accessed | tf_op | source)
XLA Modules:
  0.0 24.5 jit_solution(1159687281944393058)
XLA Ops:
  1.3 19.3 %exchange.1 = (f32[12,12,8,128]{3,2,1,0:T(8,128)S(1)}, f32[12,12,1,128]{3,2,1,0:T(1,128)S(1)}, f32[12,12,8,128]{3,2,1,0:T(8,128)S(1)}, f32[512,128]{1,0:T(8,128)...) custom-call(f32[5,8,8,128]{3,2,1,0:T(8,128)} %species.1, f32[3,8,8,128]{3,2,1,0:T(8,128)} %velocity.1, ...), custom_call_target="tpu_custom_call" | custom-call | tf_op jit(solution)/shard_map/exchange/pallas_call | solution.py:377
  20.5 3.9 %stencil.1 = (f32[320,128]{1,0:T(8,128)}, f32[192,128]{1,0:T(8,128)}, f32[16,2048]{1,0:T(8,128)}, f32[4,16,64]{2,1,0:T(8,128)}) custom-call(f32[12,12,8,128]{3,2,1,0:T(8,128)S(1)} %get-tuple-element.14.ext, f32[12,12,1,128]{3,2,1,0:T(1,128)S(1)} %get-tuple-element.15.base, f32[12,12,8,128]{3,2,1,0:T(8,128)S(1)} %get-tuple-element.16.own_start, ...), custom_call_target="tpu_custom_call" | custom-call | tf_op jit(solution)/shard_map/stencil/pallas_call | solution.py:397

commit v2 on v1

v2 whole, which is shorter than its diff:
```python
import functools

import jax
import jax.numpy as jnp
from jax import lax
from jax.experimental import pallas as pl
from jax.experimental.pallas import tpu as pltpu
from jax.sharding import PartitionSpec as P

MESH = pl.DeviceIdType.MESH
F32, BF16, I32 = jnp.float32, jnp.bfloat16, jnp.int32
time_step = 0.1
CHUNK = 512
TRIPS = (
    ((0, 1), (2, 1, 8, 2), (2, 0)), ((0, 1), (9, 1, 8, 2), (9, 0)), ((0, 1), (3, 6, 8, 2), (3, 0)),
    ((0, -1), (2, 1, 2, 2), (2, 10)), ((0, -1), (9, 1, 2, 2), (9, 10)), ((0, -1), (3, 6, 2, 2), (3, 10)),
    ((1, 0), (8, 2, 2, 8), (0, 2)), ((-1, 0), (2, 2, 2, 8), (10, 2)),
    ((1, 0), (9, 1, 1, 1), (1, 1)), ((-1, 0), (2, 1, 1, 1), (10, 1)),
    ((1, 0), (9, 1, 10, 1), (1, 10)), ((-1, 0), (2, 1, 10, 1), (10, 10)),
)
GROUP = 4
FACES = ((1, 0), (-1, 0), (0, 1), (0, -1))


def coefficient(values, base):
    row = lax.broadcasted_iota(I32, (8, 128), 0)
    kinetic = jnp.where(row >= 5, values * values, 0.0)
    for shift in (4, 2, 1):
        kinetic = kinetic + pltpu.roll(kinetic, shift, 0)
    return base * (1.0 + 0.5 * jnp.tanh(0.5 * kinetic))


def pieces(x):
    high = x.astype(BF16)
    rest = x - high.astype(F32)
    middle = rest.astype(BF16)
    low = (rest - middle.astype(F32)).astype(BF16)
    return high, middle, low


def one_hot(rows, index):
    row = lax.broadcasted_iota(I32, (rows, index.shape[1]), 0)
    return jnp.where(row == index, 1.0, 0.0).astype(BF16)


def dot_nt(a, b):
    return lax.dot_general(a, b, (((1,), (1,)), ((), ())), preferred_element_type=F32)


def z_up(x):
    lane = lax.broadcasted_iota(I32, (8, 128), 1)
    return jnp.where(lane == 127, 0.0, pltpu.roll(x, 127, 1))


class Patch:
    def __init__(self, field, coef, x, column):
        self.field, self.coef, self.x, self.column, self.kept = field, coef, x, column, {}

    def keep(self, key, make):
        if key not in self.kept:
            self.kept[key] = make()
        return self.kept[key]

    def value(self, dx, p):
        return self.keep(("v", dx, p), lambda: self.field[self.x + dx, self.column(p)])

    def own(self, dx, p):
        return self.keep(("c", dx, p), lambda: self.coef[self.x + dx, self.column(p)])

    def flux(self, dx, p, to_x, to_p):
        return self.keep(
            ("f", dx, p, to_x, to_p),
            lambda: (self.own(dx, p) + self.own(to_x, to_p)) * (self.value(to_x, to_p) - self.value(dx, p)),
        )

    def twice_change(self, dx, p):
        lane = lax.broadcasted_iota(I32, (8, 128), 1)
        value, own = self.value(dx, p), self.own(dx, p)
        up = (own + z_up(own)) * (z_up(value) - value)
        down = jnp.where(lane == 0, own * value, pltpu.roll(up, 1, 1))
        flux_x = self.flux(dx, p, dx + 1, p) - self.flux(dx - 1, p, dx, p)
        flux_y = self.flux(dx, p, dx, p + 1) - self.flux(dx, p - 1, dx, p)
        return flux_x + flux_y + (up - down)


def spray_kernel(
    n_a, n_r, species, velocity, diffusivity, parcels, cnt, cells, slots, faces,
    result, staying, arrivals,
    ext, base, start, first, later, source,
    vel, par, cel, slo, fac, vel3, leaving, outgoing,
    load_sem, send_sem, recv_sem, base_send, base_recv, row_send, row_recv,
):
    a, r = lax.axis_index("axial"), lax.axis_index("radial")
    high_late = lax.rem(r, GROUP) >= GROUP // 2
    opener = jnp.logical_and(a == 0, r == 0)

    def there(step_a, step_r):
        ok = None
        for step, at, size in ((step_a, a, n_a), (step_r, r, n_r)):
            if step:
                here = at < size - 1 if step > 0 else at > 0
                ok = here if ok is None else jnp.logical_and(ok, here)
        return ok

    barrier = pltpu.get_barrier_semaphore()
    total = jnp.int32(0)
    for da, dr in FACES:
        ok = there(da, dr)
        total = total + ok.astype(I32)

        @pl.when(ok)
        def _(da=da, dr=dr):
            pl.semaphore_signal(barrier, inc=1, device_id=(a + da, r + dr), device_id_type=MESH)

    loads = [pltpu.make_async_copy(species.at[f], ext.at[2:10, 2:10, f], load_sem.at[f]) for f in range(5)]
    loads += [pltpu.make_async_copy(velocity.at[k], ext.at[2:10, 2:10, 5 + k], load_sem.at[5 + k]) for k in range(3)]
    loads.append(pltpu.make_async_copy(diffusivity, base.at[2:10, 2:10, 0], load_sem.at[8]))
    own_loads = len(loads)
    for k, (src, dst) in enumerate(
        ((velocity, vel), (parcels, par), (cells, cel), (slots, slo), (faces, fac))
    ):
        loads.append(pltpu.make_async_copy(src, dst, load_sem.at[9 + k]))
    for load in loads:
        load.start()

    zero2 = jnp.zeros((2, 8, 8, 128), F32)
    zero3 = jnp.zeros((8, 2, 8, 128), F32)
    corner = jnp.zeros((8, 128), F32)

    def clear_corner(x, y):
        ext[x, y] = corner
        base[x, y] = corner[:1]

    @pl.when(a == 0)
    def _():
        ext[0:2, 2:10] = zero2
        base[0:2, 2:10] = zero2[:, :, :1]
        arrivals[0] = jnp.zeros((16, 64), F32)
        clear_corner(1, 1)
        clear_corner(1, 10)

    @pl.when(a == n_a - 1)
    def _():
        ext[10:12, 2:10] = zero2
        base[10:12, 2:10] = zero2[:, :, :1]
        arrivals[1] = jnp.zeros((16, 64), F32)
        clear_corner(10, 1)
        clear_corner(10, 10)

    @pl.when(r == 0)
    def _():
        ext[2:10, 0:2] = zero3
        base[2:10, 0:2] = zero3[:, :, :1]
        arrivals[2] = jnp.zeros((16, 64), F32)
        clear_corner(1, 1)
        clear_corner(10, 1)

    @pl.when(r == n_r - 1)
    def _():
        ext[2:10, 10:12] = zero3
        base[2:10, 10:12] = zero3[:, :, :1]
        arrivals[3] = jnp.zeros((16, 64), F32)
        clear_corner(1, 10)
        clear_corner(10, 10)

    source[...] = jnp.zeros((512, 128), F32)

    def gas_at(cell):
        width = cell.shape[1]
        depth_hot = one_hot(128, cell & 127)
        rows = jnp.dot(vel3[...], jnp.concatenate([depth_hot] * 3, axis=0), preferred_element_type=F32)
        here = lax.broadcasted_iota(I32, (64, width), 0) == (cell >> 7)
        gas = [
            jnp.sum(jnp.where(here, rows[64 * k : 64 * k + 64], 0.0), axis=0, keepdims=True) for k in range(3)
        ]
        return jnp.concatenate(gas, axis=0), here, depth_hot

    def push(old, gas):
        drag = old[4:5] * (gas - old[0:3])
        new_velocity = old[0:3] + time_step * drag
        new_mass = old[3:4] * (1.0 - time_step * old[5:6])
        new_position = old[6:9] + time_step * new_velocity
        return drag, jnp.concatenate([new_velocity, new_mass, old[4:6], new_position, old[9:16]], axis=0)

    def find_leavers():
        vel3[...] = jnp.concatenate(pieces(vel[...].reshape(192, 128)), axis=1)
        lane_cells = [cel[:, 128 * h : 128 * h + 128].astype(F32) for h in range(16)]
        stacked = jnp.concatenate([par[:, 128 * h : 128 * h + 128] for h in range(16)] + lane_cells, axis=0)
        stacked3 = jnp.concatenate(pieces(stacked), axis=1)
        leave_sum = jnp.zeros((16, 128), F32)
        moved, moved_cells = [], []
        for f in range(4):
            member = lax.broadcasted_iota(I32, (1, 64), 1)
            slot = jnp.where(member < fac[0:1, f : f + 1], slo[f : f + 1, :], -1)
            high, low_hot = slot >> 7, one_hot(128, slot & 127)
            leave_sum = leave_sum + dot_nt(one_hot(16, high), low_hot)
            picked = jnp.dot(stacked3, jnp.concatenate([low_hot] * 3, axis=0), preferred_element_type=F32)
            out = jnp.zeros((16, 64), F32)
            for h in range(16):
                out = out + jnp.where(high == h, picked[16 * h : 16 * h + 16], 0.0)
            chosen = lax.broadcasted_iota(I32, (16, 64), 0) == high
            moved.append(out)
            moved_cells.append(jnp.sum(jnp.where(chosen, picked[256:272], 0.0), axis=0, keepdims=True))
        leaving[...] = leave_sum

        for f in range(4):
            gas, _, _ = gas_at(moved_cells[f].astype(I32))
            member = lax.broadcasted_iota(I32, (1, 64), 1)
            outgoing[f] = jnp.where(member < fac[0:1, f : f + 1], push(moved[f], gas)[1], 0.0)

    def parcel_step(c, _):
        span = pl.ds(pl.multiple_of(c * CHUNK, CHUNK), CHUNK)
        gas, here, depth_hot = gas_at(cel[:, span])
        old = par[:, span]
        mass, evaporation = old[3:4], old[5:6]
        drag, new = push(old, gas)
        live = lax.broadcasted_iota(I32, (1, CHUNK), 1) + c * CHUNK < cnt[0, 0]
        leave = jnp.concatenate(
            [leaving[pl.ds(c * (CHUNK // 128) + j, 1), :] for j in range(CHUNK // 128)], axis=1
        )
        staying[:, span] = jnp.where(jnp.logical_and(live, leave == 0.0), new, 0.0)
        deposit = [mass * evaporation] + [-mass * drag[k : k + 1] for k in range(3)]
        split = [pieces(jnp.where(live, d, 0.0)) for d in deposit]
        added = jnp.zeros((256, 128), F32)
        for p in range(3):
            spread = jnp.concatenate(
                [jnp.where(here, split[k][p].astype(F32), 0.0).astype(BF16) for k in range(4)], axis=0
            )
            added = added + dot_nt(spread, depth_hot)
        source[0:64] += added[0:64]
        source[320:512] += added[64:256]
        return 0

    for load in loads:
        load.wait()

    chunks = 2048 // CHUNK
    ahead = jnp.where(opener, 0, chunks)
    pl.when(jnp.logical_not(opener))(find_leavers)
    lax.fori_loop(0, ahead, parcel_step, 0)

    pl.semaphore_wait(barrier, total)

    def trip(k):
        (da, dr), (sx, nx, sy, ny), (tx, ty) = TRIPS[k]
        device = (a + da, r + dr)
        return (
            pltpu.make_async_remote_copy(
                src_ref=ext.at[sx : sx + nx, sy : sy + ny],
                dst_ref=ext.at[tx : tx + nx, ty : ty + ny],
                send_sem=send_sem.at[k], recv_sem=recv_sem.at[k],
                device_id=device, device_id_type=MESH,
            ),
            pltpu.make_async_remote_copy(
                src_ref=base.at[sx : sx + nx, sy : sy + ny],
                dst_ref=base.at[tx : tx + nx, ty : ty + ny],
                send_sem=base_send.at[k], recv_sem=base_recv.at[k],
                device_id=device, device_id_type=MESH,
            ),
        )

    def sends(k):
        da, dr = TRIPS[k][0]
        out, back = there(da, dr), there(-da, -dr)
        if k >= 8:
            side = there(0, -1) if k < 10 else there(0, 1)
            out, back = jnp.logical_and(out, side), jnp.logical_and(back, side)
        return out, back

    def send(trips, ok=None):
        for k in trips:
            out, _ = sends(k)

            @pl.when(out if ok is None else jnp.logical_and(out, ok))
            def _(k=k):
                for copy in trip(k):
                    copy.start()

    def receive(trips, ok=None):
        for k in trips:
            _, back = sends(k)

            @pl.when(back if ok is None else jnp.logical_and(back, ok))
            def _(k=k):
                for copy in trip(k):
                    copy.wait_recv()

    to_high, to_low = lax.rem(r, GROUP) == GROUP - 1, lax.rem(r, GROUP) == 0
    send((0, 1, 2), to_high)
    send((3, 4, 5), to_low)
    send((6, 7))
    send((0, 1, 2), jnp.logical_not(to_high))
    send((3, 4, 5), jnp.logical_not(to_low))

    def row_copy(f):
        da, dr = FACES[f]
        return pltpu.make_async_remote_copy(
            src_ref=outgoing.at[f], dst_ref=arrivals.at[f],
            send_sem=row_send.at[f], recv_sem=row_recv.at[f],
            device_id=(a + da, r + dr), device_id_type=MESH,
        )

    def send_rows(ok):
        for f in (2, 3, 0, 1):

            @pl.when(jnp.logical_and(there(*FACES[f]), ok))
            def _(f=f):
                row_copy(f).start()

    send_rows(jnp.logical_not(opener))

    pl.when(opener)(find_leavers)

    def own_start(x, _):
        for y in range(2, 10):
            start[x, y] = coefficient(ext[x, y], base[x, y])
        return 0

    lax.fori_loop(2, 10, own_start, 0)
    send_rows(opener)
    low_late = jnp.logical_not(high_late)
    receive((0, 1), high_late)
    send((8, 9), high_late)
    receive((3, 4), low_late)
    send((10, 11), low_late)
    receive((3, 4), high_late)
    send((10, 11), high_late)
    receive((0, 1), low_late)
    send((8, 9), low_late)

    lax.fori_loop(ahead, chunks, parcel_step, 0)

    def find_start(x, y):
        start[x, y] = coefficient(ext[x, y], base[x, y])

    def find_first(patch, dx, p, outside):
        x, y = patch.x + dx, patch.column(p)
        new = patch.value(dx, p) + (0.5 * time_step) * patch.twice_change(dx, p)
        if outside is not None:
            new = jnp.where(outside, 0.0, new)
        first[x, y] = new
        later[x, y] = coefficient(new, base[x, y])

    def find_second(patch, dx, p):
        x, y = patch.x + dx, patch.column(p)
        cell = (x - 2) * 8 + (y - 2)
        result[pl.ds(cell, 8, stride=64), :] = (
            0.5 * (ext[x, y] + patch.value(dx, p))
            + (0.25 * time_step) * patch.twice_change(dx, p)
            + time_step * source[pl.ds(cell, 8, stride=64), :]
        )

    def repeat(low, high, step):
        def run(i, _):
            step(i)
            return 0

        lax.fori_loop(low, high, run, 0)

    def inner_first(x):
        patch = Patch(ext, start, x, lambda p: p)
        for p in range(3, 9):
            find_first(patch, 0, p, None)

    def inner_second(x):
        patch = Patch(first, later, x, lambda p: p)
        for p in range(4, 8):
            find_second(patch, 0, p)

    repeat(3, 9, inner_first)
    repeat(4, 8, inner_second)

    places = [jnp.where(high_late, p, 11 - p) for p in range(12)]

    def column(p):
        return places[p]

    early_edge = jnp.where(high_late, r == 0, r == n_r - 1)
    late_edge = jnp.where(high_late, r == n_r - 1, r == 0)

    receive((6, 7))
    receive((2, 8, 9), high_late)
    receive((5, 10, 11), low_late)

    def early_side_start(i):
        for dx in range(4):
            for p in (0, 1):
                find_start(2 + 4 * i + dx, column(p))

    def early_end_start(i):
        for p in range(2, 10):
            find_start(11 * i, column(p))
        for p in range(1, 10):
            find_start(1 + 9 * i, column(p))

    repeat(0, 2, early_side_start)
    repeat(0, 2, early_end_start)

    def early_end_first(i):
        outer = Patch(ext, start, 1 + 9 * i, column)
        for p in range(2, 9):
            find_first(outer, 0, p, jnp.where(i == 0, a == 0, a == n_a - 1))
        inner = Patch(ext, start, 2 + 7 * i, column)
        for p in range(1, 9):
            find_first(inner, 0, p, early_edge if p == 1 else None)

    def early_side_first(i):
        patch = Patch(ext, start, 3 + 3 * i, column)
        for dx in range(3):
            find_first(patch, dx, 1, early_edge)
            find_first(patch, dx, 2, None)

    repeat(0, 2, early_end_first)
    repeat(0, 2, early_side_first)

    def early_end_second(i):
        patch = Patch(first, later, 2 + 6 * i, column)
        for dx in (0, 1):
            for p in range(2, 8):
                find_second(patch, dx, p)

    def early_side_second(i):
        patch = Patch(first, later, 4 + 2 * i, column)
        for dx in (0, 1):
            for p in (2, 3):
                find_second(patch, dx, p)

    repeat(0, 2, early_end_second)
    repeat(0, 2, early_side_second)

    for f, (da, dr) in enumerate(FACES):

        @pl.when(there(-da, -dr))
        def _(f=f):
            row_copy(f).wait_recv()

    for k in range(12):

        @pl.when(sends(k)[0])
        def _(k=k):
            for copy in trip(k):
                copy.wait_send()

    for f, (da, dr) in enumerate(FACES):

        @pl.when(there(da, dr))
        def _(f=f):
            row_copy(f).wait_send()

    receive((5, 10, 11), high_late)
    receive((2, 8, 9), low_late)

    for x in range(2, 10):
        for p in (10, 11):
            find_start(x, column(p))
    for x in (1, 10):
        find_start(x, column(10))
    patch = Patch(ext, start, 0, column)
    find_first(patch, 1, 9, a == 0)
    for x in range(2, 10):
        find_first(patch, x, 9, None)
        find_first(patch, x, 10, late_edge)
    find_first(patch, 10, 9, a == n_a - 1)
    patch = Patch(first, later, 0, column)
    for x in range(2, 10):
        for p in (8, 9):
            find_second(patch, x, p)


def store_kernel(result, staying, arrivals, species_out, velocity_out, staying_out, arrivals_out, sems):
    copies = [
        pltpu.make_async_copy(src, dst, sems.at[k])
        for k, (src, dst) in enumerate(
            (
                (result.at[0:320], species_out), (result.at[320:512], velocity_out),
                (staying, staying_out), (arrivals, arrivals_out),
            )
        )
    ]
    for copy in copies:
        copy.start()
    for copy in copies:
        copy.wait()


def body(n_a, n_r, species, velocity, diffusivity, parcels, counts, cells, leave_slots, leave_counts):
    anywhere = pl.BlockSpec(memory_space=pl.ANY)
    vmem = pl.BlockSpec(memory_space=pltpu.VMEM)
    shape = lambda *dims: jax.ShapeDtypeStruct(dims, F32)
    local = lambda *dims: pltpu.VMEM(dims, F32)
    dma = pltpu.SemaphoreType.DMA
    between = pl.pallas_call(
        functools.partial(spray_kernel, n_a, n_r),
        name="spray",
        out_shape=[local(512, 128), local(16, 2048), local(4, 16, 64)],
        in_specs=[anywhere] * 4 + [pl.BlockSpec(memory_space=pltpu.SMEM)] + [anywhere] * 3,
        out_specs=[vmem] * 3,
        scratch_shapes=[
            local(12, 12, 8, 128), local(12, 12, 1, 128), local(12, 12, 8, 128), local(12, 12, 8, 128),
            local(12, 12, 8, 128), local(512, 128),
            local(3, 8, 8, 128), local(16, 2048),
            pltpu.VMEM((1, 2048), I32), pltpu.VMEM((4, 64), I32), pltpu.VMEM((1, 4), I32),
            pltpu.VMEM((192, 384), BF16), local(16, 128), local(4, 16, 64),
            dma((14,)), dma((12,)), dma((12,)), dma((12,)), dma((12,)), dma((4,)), dma((4,)),
        ],
        compiler_params=pltpu.CompilerParams(collective_id=0, has_side_effects=True),
    )(
        species, velocity, diffusivity, parcels[0, 0], counts, cells[0], leave_slots[0, 0], leave_counts[0],
    )
    species_out, velocity_out, staying, arrivals = pl.pallas_call(
        store_kernel,
        name="store",
        out_shape=[shape(320, 128), shape(192, 128), shape(16, 2048), shape(4, 16, 64)],
        in_specs=[vmem] * 3,
        out_specs=[anywhere] * 4,
        scratch_shapes=[dma((4,))],
    )(*[pltpu.with_memory_space_constraint(x, pltpu.VMEM) for x in between])
    return (
        species_out.reshape(5, 8, 8, 128), velocity_out.reshape(3, 8, 8, 128),
        staying[None, None], arrivals[None, None],
    )


def solution(mesh):
    return jax.shard_map(
        functools.partial(body, mesh.shape["axial"], mesh.shape["radial"]),
        mesh=mesh,
        in_specs=(
            P(None, "axial", "radial", None),
            P(None, "axial", "radial", None),
            P("axial", "radial", None),
            P("axial", "radial", None, None),
            P("axial", "radial"),
            P("axial", "radial", None),
            P("axial", "radial", None, None),
            P("axial", "radial", None),
        ),
        out_specs=(
            P(None, "axial", "radial", None),
            P(None, "axial", "radial", None),
            P("axial", "radial", None, None),
            P("axial", "radial", None, None, None),
        ),
        check_vma=False,
    )
```

time: 24.6 us -> 22.4 us (0.911)
  the two profiles are of different devices: /device:TPU:255 before, /device:TPU:287 now
where the time goes in v2:
time: 22.4 us; the launch traced here: 22.2 us
  Pallas kernels  20.9 us (93%)
  between operations  1.29 us (6%)
    pallas_call x1, Pallas kernels, body(): pl.pallas_call(functools.partial(spray_kernel, n_a, n_r), name='spray', o...  20.2 us
    pallas_call x1, Pallas kernels, body(): pl.pallas_call(store_kernel, name='store', out_shape=[shape(320, 128), sh...  0.78 us

profile of v2, /device:TPU:287, one launch (start us, length us, event | category | flops | bytes accessed | tf_op | source)
XLA Modules:
  0.0 22.2 jit_solution(17958772265140023732)
XLA Ops:
  1.3 20.2 %spray.1 = (f32[512,128]{1,0:T(8,128)S(1)}, f32[16,2048]{1,0:T(8,128)S(1)}, f32[4,16,64]{2,1,0:T(8,128)S(1)}) custom-call(f32[5,8,8,128]{3,2,1,0:T(8,128)} %species.1, f32[3,8,8,128]{3,2,1,0:T(8,128)} %velocity.1, f32[8,8,128]{2,1,0:T(8,128)} %diffusivity.1, f32[16,2048]{1,0:T(8,128)} %bitcast.8, s32[1,1]{1,0:T(1,128)S(6)} %copy.12.cnt, s32[1,2048]{1,0:T(1,128)} %bitcast.9, ...), custom_call_target="tpu_custom_call" | custom-call | tf_op jit(solution)/shard_map/spray/pallas_call | solution.py:492
  21.4 0.8 %store.1 = (f32[320,128]{1,0:T(8,128)}, f32[192,128]{1,0:T(8,128)}, f32[16,2048]{1,0:T(8,128)}, f32[4,16,64]{2,1,0:T(8,128)}) custom-call(f32[512,128]{1,0:T(8,128)S(1)} %get-tuple-element.11.result, f32[16,2048]{1,0:T(8,128)S(1)} %get-tuple-element.12.staying, f32[4,16,64]{2,1,0:T(8,128)S(1)} %get-tuple-element.13.arrivals), custom_call_target="tpu_custom_call" | custom-call | tf_op jit(solution)/shard_map/store/pallas_call | solution.py:510

commit v3 on v2

--- a/solution.py
+++ b/solution.py
@@ -92,7 +92,10 @@
 ):
     a, r = lax.axis_index("axial"), lax.axis_index("radial")
     high_late = lax.rem(r, GROUP) >= GROUP // 2
+    in_group = lax.rem(r, GROUP)
+    inside = jnp.logical_and(in_group != GROUP - 1, jnp.logical_and(lax.rem(a, 2) == 0, a > 0))
     opener = jnp.logical_and(a == 0, r == 0)
+    eager = jnp.logical_or(jnp.logical_or(jnp.logical_and(in_group == 0, r > 0), inside), opener)
 
     def there(step_a, step_r):
         ok = None
@@ -235,8 +238,8 @@
         load.wait()
 
     chunks = 2048 // CHUNK
-    ahead = jnp.where(opener, 0, chunks)
-    pl.when(jnp.logical_not(opener))(find_leavers)
+    ahead = jnp.where(eager, 0, chunks)
+    pl.when(jnp.logical_not(eager))(find_leavers)
     lax.fori_loop(0, ahead, parcel_step, 0)
 
     pl.semaphore_wait(barrier, total)
@@ -307,9 +310,9 @@
             def _(f=f):
                 row_copy(f).start()
 
-    send_rows(jnp.logical_not(opener))
-
-    pl.when(opener)(find_leavers)
+    send_rows(jnp.logical_not(eager))
+
+    pl.when(eager)(find_leavers)
 
     def own_start(x, _):
         for y in range(2, 10):
@@ -317,17 +320,16 @@
         return 0
 
     lax.fori_loop(2, 10, own_start, 0)
-    send_rows(opener)
+    send_rows(eager)
     low_late = jnp.logical_not(high_late)
-    receive((0, 1), high_late)
-    send((8, 9), high_late)
-    receive((3, 4), low_late)
-    send((10, 11), low_late)
-    receive((3, 4), high_late)
-    send((10, 11), high_late)
-    receive((0, 1), low_late)
-    send((8, 9), low_late)
-
+
+    def hand_on(ok, early):
+        for is_high in (False, True):
+            chosen = jnp.logical_and(ok, low_late if is_high == early else high_late)
+            receive((3, 4) if is_high else (0, 1), chosen)
+            send((10, 11) if is_high else (8, 9), chosen)
+
+    hand_on(eager, True)
     lax.fori_loop(ahead, chunks, parcel_step, 0)
 
     def find_start(x, y):
@@ -369,6 +371,8 @@
 
     repeat(3, 9, inner_first)
     repeat(4, 8, inner_second)
+    hand_on(jnp.logical_not(eager), True)
+    hand_on(jnp.bool_(True), False)
 
     places = [jnp.where(high_late, p, 11 - p) for p in range(12)]
 

time: 22.4 us -> 21 us (0.938)
  the two profiles are of different devices: /device:TPU:287 before, /device:TPU:518 now
where the time goes in v3:
time: 21 us; the launch traced here: 20.9 us
  Pallas kernels  19.6 us (93%)
  between operations  1.29 us (6%)
    pallas_call x1, Pallas kernels, body(): pl.pallas_call(functools.partial(spray_kernel, n_a, n_r), name='spray', o...  18.8 us
    pallas_call x1, Pallas kernels, body(): pl.pallas_call(store_kernel, name='store', out_shape=[shape(320, 128), sh...  0.78 us

profile of v3, /device:TPU:518, one launch (start us, length us, event | category | flops | bytes accessed | tf_op | source)
XLA Modules:
  0.0 20.9 jit_solution(16478000580022783981)
XLA Ops:
  1.3 18.8 %spray.1 = (f32[512,128]{1,0:T(8,128)S(1)}, f32[16,2048]{1,0:T(8,128)S(1)}, f32[4,16,64]{2,1,0:T(8,128)S(1)}) custom-call(f32[5,8,8,128]{3,2,1,0:T(8,128)} %species.1, f32[3,8,8,128]{3,2,1,0:T(8,128)} %velocity.1, f32[8,8,128]{2,1,0:T(8,128)} %diffusivity.1, f32[16,2048]{1,0:T(8,128)} %bitcast.8, s32[1,1]{1,0:T(1,128)S(6)} %copy.12.cnt, s32[1,2048]{1,0:T(1,128)} %bitcast.9, ...), custom_call_target="tpu_custom_call" | custom-call | tf_op jit(solution)/shard_map/spray/pallas_call | solution.py:496
  20.1 0.8 %store.1 = (f32[320,128]{1,0:T(8,128)}, f32[192,128]{1,0:T(8,128)}, f32[16,2048]{1,0:T(8,128)}, f32[4,16,64]{2,1,0:T(8,128)}) custom-call(f32[512,128]{1,0:T(8,128)S(1)} %get-tuple-element.11.result, f32[16,2048]{1,0:T(8,128)S(1)} %get-tuple-element.12.staying, f32[4,16,64]{2,1,0:T(8,128)S(1)} %get-tuple-element.13.arrivals), custom_call_target="tpu_custom_call" | custom-call | tf_op jit(solution)/shard_map/store/pallas_call | solution.py:514

commit v4 on v3

--- a/solution.py
+++ b/solution.py
@@ -289,9 +289,12 @@
                     copy.wait_recv()
 
     to_high, to_low = lax.rem(r, GROUP) == GROUP - 1, lax.rem(r, GROUP) == 0
-    send((0, 1, 2), to_high)
-    send((3, 4, 5), to_low)
+    send((0, 1), to_high)
+    send((3, 4), to_low)
+    even = lax.rem(a, 2) == 0
+    send((5,), jnp.logical_and(to_low, even))
     send((6, 7))
+    send((2,), jnp.logical_and(to_high, even))
     send((0, 1, 2), jnp.logical_not(to_high))
     send((3, 4, 5), jnp.logical_not(to_low))
 
@@ -321,6 +324,8 @@
 
     lax.fori_loop(2, 10, own_start, 0)
     send_rows(eager)
+    send((2,), jnp.logical_and(to_high, jnp.logical_not(even)))
+    send((5,), jnp.logical_and(to_low, jnp.logical_not(even)))
     low_late = jnp.logical_not(high_late)
 
     def hand_on(ok, early):
@@ -431,25 +436,6 @@
 
     repeat(0, 2, early_end_second)
     repeat(0, 2, early_side_second)
-
-    for f, (da, dr) in enumerate(FACES):
-
-        @pl.when(there(-da, -dr))
-        def _(f=f):
-            row_copy(f).wait_recv()
-
-    for k in range(12):
-
-        @pl.when(sends(k)[0])
-        def _(k=k):
-            for copy in trip(k):
-                copy.wait_send()
-
-    for f, (da, dr) in enumerate(FACES):
-
-        @pl.when(there(da, dr))
-        def _(f=f):
-            row_copy(f).wait_send()
 
     receive((5, 10, 11), high_late)
     receive((2, 8, 9), low_late)
@@ -469,6 +455,25 @@
     for x in range(2, 10):
         for p in (8, 9):
             find_second(patch, x, p)
+
+    for f, (da, dr) in enumerate(FACES):
+
+        @pl.when(there(-da, -dr))
+        def _(f=f):
+            row_copy(f).wait_recv()
+
+    for k in range(12):
+
+        @pl.when(sends(k)[0])
+        def _(k=k):
+            for copy in trip(k):
+                copy.wait_send()
+
+    for f, (da, dr) in enumerate(FACES):
+
+        @pl.when(there(da, dr))
+        def _(f=f):
+            row_copy(f).wait_send()
 
 
 def store_kernel(result, staying, arrivals, species_out, velocity_out, staying_out, arrivals_out, sems):

time: 21 us -> 21.1 us (level)
  the two profiles are of different devices: /device:TPU:518 before, /device:TPU:512 now
where the time goes in v4:
time: 21.1 us; the launch traced here: 20.9 us
  Pallas kernels  19.6 us (93%)
  between operations  1.29 us (6%)
    pallas_call x1, Pallas kernels, body(): pl.pallas_call(functools.partial(spray_kernel, n_a, n_r), name='spray', o...  18.8 us
    pallas_call x1, Pallas kernels, body(): pl.pallas_call(store_kernel, name='store', out_shape=[shape(320, 128), sh...  0.78 us

profile of v4, /device:TPU:512, one launch (start us, length us, event | category | flops | bytes accessed | tf_op | source)
XLA Modules:
  0.0 20.9 jit_solution(1217472834115806158)
XLA Ops:
  1.3 18.8 %spray.1 = (f32[512,128]{1,0:T(8,128)S(1)}, f32[16,2048]{1,0:T(8,128)S(1)}, f32[4,16,64]{2,1,0:T(8,128)S(1)}) custom-call(f32[5,8,8,128]{3,2,1,0:T(8,128)} %species.1, f32[3,8,8,128]{3,2,1,0:T(8,128)} %velocity.1, f32[8,8,128]{2,1,0:T(8,128)} %diffusivity.1, f32[16,2048]{1,0:T(8,128)} %bitcast.8, s32[1,1]{1,0:T(1,128)S(6)} %copy.12.cnt, s32[1,2048]{1,0:T(1,128)} %bitcast.9, ...), custom_call_target="tpu_custom_call" | custom-call | tf_op jit(solution)/shard_map/spray/pallas_call | solution.py:501
  20.1 0.8 %store.1 = (f32[320,128]{1,0:T(8,128)}, f32[192,128]{1,0:T(8,128)}, f32[16,2048]{1,0:T(8,128)}, f32[4,16,64]{2,1,0:T(8,128)}) custom-call(f32[512,128]{1,0:T(8,128)S(1)} %get-tuple-element.11.result, f32[16,2048]{1,0:T(8,128)S(1)} %get-tuple-element.12.staying, f32[4,16,64]{2,1,0:T(8,128)S(1)} %get-tuple-element.13.arrivals), custom_call_target="tpu_custom_call" | custom-call | tf_op jit(solution)/shard_map/store/pallas_call | solution.py:519

commit v5 on v4

--- a/solution.py
+++ b/solution.py
@@ -377,7 +377,7 @@
     repeat(3, 9, inner_first)
     repeat(4, 8, inner_second)
     hand_on(jnp.logical_not(eager), True)
-    hand_on(jnp.bool_(True), False)
+    hand_on(jnp.logical_not(even), False)
 
     places = [jnp.where(high_late, p, 11 - p) for p in range(12)]
 
@@ -437,6 +437,7 @@
     repeat(0, 2, early_end_second)
     repeat(0, 2, early_side_second)
 
+    hand_on(even, False)
     receive((5, 10, 11), high_late)
     receive((2, 8, 9), low_late)
 

time: 21.1 us -> 25.4 us (1.20)
  the two profiles are of different devices: /device:TPU:512 before, /device:TPU:255 now
where the time goes in v5:
time: 25.4 us; the launch traced here: 25.2 us
  Pallas kernels  23.9 us (94%)
  between operations  1.29 us (5%)
    pallas_call x1, Pallas kernels, body(): pl.pallas_call(functools.partial(spray_kernel, n_a, n_r), name='spray', o...  23.1 us
    pallas_call x1, Pallas kernels, body(): pl.pallas_call(store_kernel, name='store', out_shape=[shape(320, 128), sh...  0.78 us

profile of v5, /device:TPU:255, one launch (start us, length us, event | category | flops | bytes accessed | tf_op | source)
XLA Modules:
  0.0 25.2 jit_solution(16906470113300455876)
XLA Ops:
  1.3 23.1 %spray.1 = (f32[512,128]{1,0:T(8,128)S(1)}, f32[16,2048]{1,0:T(8,128)S(1)}, f32[4,16,64]{2,1,0:T(8,128)S(1)}) custom-call(f32[5,8,8,128]{3,2,1,0:T(8,128)} %species.1, f32[3,8,8,128]{3,2,1,0:T(8,128)} %velocity.1, f32[8,8,128]{2,1,0:T(8,128)} %diffusivity.1, f32[16,2048]{1,0:T(8,128)} %bitcast.8, s32[1,1]{1,0:T(1,128)S(6)} %copy.12.cnt, s32[1,2048]{1,0:T(1,128)} %bitcast.9, ...), custom_call_target="tpu_custom_call" | custom-call | tf_op jit(solution)/shard_map/spray/pallas_call | solution.py:502
  24.4 0.8 %store.1 = (f32[320,128]{1,0:T(8,128)}, f32[192,128]{1,0:T(8,128)}, f32[16,2048]{1,0:T(8,128)}, f32[4,16,64]{2,1,0:T(8,128)}) custom-call(f32[512,128]{1,0:T(8,128)S(1)} %get-tuple-element.11.result, f32[16,2048]{1,0:T(8,128)S(1)} %get-tuple-element.12.staying, f32[4,16,64]{2,1,0:T(8,128)S(1)} %get-tuple-element.13.arrivals), custom_call_target="tpu_custom_call" | custom-call | tf_op jit(solution)/shard_map/store/pallas_call | solution.py:520
